TPU v7x, 32 devices: a whole 2x2x4 slice. The times are simulated.
32 devices in a mesh: lat: 4 (over x, core), ch: 8 (over z, y).
Axes of the slice: x: 2, y: 2, z: 4, core: 2. Of those that a mesh axis runs over, the one named last changes fastest.
Arguments:
- field: bfloat16 [256, 1024, 2048], P('ch', 'lat'), may hold values from -6 to 6
- band: float32 [2, 5, 1024], replicated, may hold values from -1 to 1
- mixing: bfloat16 [2, 256, 256], replicated, may hold values from -0.375 to 0.375
Outputs:
- filtered: bfloat16 [256, 1024, 2048], P('ch', 'lat')
All inputs are finite; a program needn't handle non-finite values.
Results may differ from a plain program's by a relative error of at most 0.0092.
Values may be sent and summed in bfloat16 or wider, within the bound.
A program may use at most 256 MiB of HBM per device.

v0:
```python
import math

import jax
import jax.numpy as jnp
from jax import lax
from jax.sharding import PartitionSpec as P

NLAT = 1024
NLON = 2048
KM = 512
KL = 1024


def lon_wave(column, points):
    parity = column // KM
    component = column % KM // (KM // 2)
    longitude_mode = 2 * (column % (KM // 2)) + parity
    phase_angles = points[:, None] * longitude_mode[None, :] % NLON
    angles = phase_angles.astype(jnp.float32) * (2.0 * math.pi / NLON)
    wave_table = jnp.where(component[None, :] == 0, jnp.cos(angles), jnp.sin(angles)) / math.sqrt(
        NLON
    )
    weight = jnp.where(longitude_mode == 0, 1.0, 2.0).astype(jnp.float32)
    return (wave_table, weight)


def lat_table(parity):
    index_of_row = jnp.arange(NLAT, dtype=jnp.int32)
    wavenumbers = jnp.arange(KL, dtype=jnp.int32) + parity
    phase_angles = (2 * index_of_row[:, None] + 1) * wavenumbers[None, :] % (4 * NLAT)
    angles = phase_angles.astype(jnp.float32) * (math.pi / (2 * NLAT))
    wave_table = jnp.where(parity == 0, jnp.cos(angles), jnp.sin(angles))
    return (wave_table * math.sqrt(2.0 / NLAT)).astype(jnp.bfloat16)


def convert(amplitudes, coeffs):
    padded = jnp.pad(amplitudes, ((0, 0), (2, 2), (0, 0)))
    summed = coeffs[0][None, :, None] * padded[:, 0:KL, :]
    for offset in range(1, 5):
        summed = summed + coeffs[offset][None, :, None] * padded[:, offset : offset + KL, :]
    return summed


def per_device(field, band, mixing):
    lat_index = lax.axis_index("lat")
    lat_pieces = lax.axis_size("lat")
    column_all = jnp.arange(2 * KM, dtype=jnp.int32)
    points = jnp.arange(NLON, dtype=jnp.int32)
    forward_lon = lon_wave(column_all, points)[0].astype(jnp.bfloat16)
    spectra = jnp.einsum(
        "crn,nk->ckr", field, forward_lon, preferred_element_type=jnp.float32
    ).astype(jnp.bfloat16)
    lat_share = 2 * KM // lat_pieces
    parity = lat_index * lat_share // KM
    legendre_table = lat_table(parity)
    coeffs = lax.dynamic_index_in_dim(band, parity, 0, keepdims=False)
    weights = lax.dynamic_index_in_dim(mixing, parity, 0, keepdims=False)
    amplitudes = jnp.einsum(
        "xdh,hr->xrd",
        lax.all_to_all(spectra, "lat", split_axis=1, concat_axis=2, tiled=True),
        legendre_table,
        preferred_element_type=jnp.float32,
    )
    converted = convert(amplitudes, coeffs).astype(jnp.bfloat16)
    mixed = jnp.einsum(
        "zf,frn->zrn",
        weights,
        lax.all_to_all(converted, "ch", split_axis=1, concat_axis=0, tiled=True),
        preferred_element_type=jnp.float32,
    ).astype(jnp.bfloat16)
    channel_mixed_spectra = lax.all_to_all(mixed, "ch", split_axis=0, concat_axis=1, tiled=True)
    lat_rows = jnp.einsum(
        "fnb,wn->fbw", channel_mixed_spectra, legendre_table, preferred_element_type=jnp.float32
    ).astype(jnp.bfloat16)
    returned = lax.all_to_all(lat_rows, "lat", split_axis=2, concat_axis=1, tiled=True)
    inverse_wave, weight = lon_wave(column_all, points)
    longitude_inverse_transform = (inverse_wave * weight[None, :]).astype(jnp.bfloat16)
    result = jnp.einsum(
        "ckr,nk->crn", returned, longitude_inverse_transform, preferred_element_type=jnp.float32
    )
    return result.astype(jnp.bfloat16)


def solution(mesh):
    return jax.shard_map(
        per_device,
        mesh=mesh,
        in_specs=(P("ch", "lat", None), P(), P()),
        out_specs=P("ch", "lat", None),
        check_vma=False,
    )
```

profile of v0, /device:TPU:0, one launch (start us, length us, event | category | flops | bytes accessed | tf_op | source)
XLA Modules:
  0.0 1597.7 jit_solution(10854917608585430571)
XLA Ops:
  1.2 34.8 %fusion.82 = bf16[2048,1024,1]{1,0,2:T(8,128)(2,1)} fusion(s32[1024]{0:T(1024)S(1)} %fusion.33, pred[1024]{0:T(1024)(128)(4,1)S(1)} %fusion.32), kind=kLoop, calls=%fused_computation.30.clone.clone.1 | loop fusion | flops 35651584 | bytes 4199424 | tf_op jit(solution)/shard_map/crn,nk->ckr/dot_general | solution.py:50
  36.0 42.1 %convert_bitcast_fusion = bf16[32,1024,256]{2,1,0:T(8,128)(2,1)} fusion(bf16[32,256,2048]{2,1,0:T(8,128)(2,1)} %param.3, bf16[2048,1024,1]{1,0,2:T(8,128)(2,1)} %fusion.82), kind=kOutput, calls=%fused_computation.6 | convolution fusion | flops 34368126976 | bytes 54525952 | tf_op jit(solution)/shard_map/crn,nk->ckr/dot_general | solution.py:50
  78.1 18.3 %copy.11 = bf16[32,1024,256]{2,0,1:T(8,128)(2,1)} copy(bf16[32,1024,256]{2,1,0:T(8,128)(2,1)} %convert_bitcast_fusion) | data formatting | bytes 33554432 | tf_op jit(solution)/shard_map/convert_element_type | solution.py:52
  103.6 17.5 %fusion.84 = bf16[1024,1024,1]{1,0,2:T(8,128)(2,1)S(1)} fusion(s32[1024]{0:T(1024)S(1)} %get-tuple-element.10, s32[1024]{0:T(1024)S(1)} %get-tuple-element.11, pred[]{:T(512)S(6)} %eq.32), kind=kLoop, calls=%fused_computation.35.clone.1.clone.1 | loop fusion | flops 17825792 | bytes 2105345 | tf_op jit(solution)/shard_map/xdh,hr->xrd/dot_general | solution.py:58
  121.1 166.0 %all-to-all-done = bf16[32,1024,256]{2,0,1:T(8,128)(2,1)} async-done(((bf16[32,1024,256]{2,0,1:T(8,128)(2,1)}), bf16[32,1024,256]{2,0,1:T(8,128)(2,1)}, u32[]{:S(2)}, u32[]{:S(2)}) %all-to-all-start) | async-done | bytes 16777248 | tf_op jit(solution)/shard_map/all_to_all | solution.py:60
  287.2 22.3 %copy.27 = bf16[32,4,256,256]{3,1,2,0:T(4,128)(2,1)} copy(bf16[32,4,256,256]{3,0,2,1:T(8,128)(2,1)} %bitcast.6) | data formatting | bytes 33554432 | tf_op jit(solution)/shard_map/all_to_all | solution.py:60
  309.4 27.3 %all_to_all.55 = bf16[32,256,1024]{2,1,0:T(8,128)(2,1)} reshape(bf16[32,256,4,256]{3,2,1,0:T(4,128)(2,1)} %bitcast.72) | data formatting | bytes 33554432 | tf_op jit(solution)/shard_map/all_to_all | solution.py:60
  336.8 25.5 %convolution_bitcast_fusion = f32[32,1024,256]{2,1,0:T(8,128)} fusion(bf16[32,256,1024]{2,1,0:T(8,128)(2,1)} %all_to_all.55, bf16[1024,1024,1]{1,0,2:T(8,128)(2,1)S(1)} %fusion.84), kind=kOutput, calls=%fused_computation.7 | convolution fusion | flops 17179869184 | bytes 52428800 | tf_op jit(solution)/shard_map/xdh,hr->xrd/dot_general | solution.py:58
  362.3 59.1 %add_convert_fusion = bf16[32,1024,256]{2,1,0:T(8,128)(2,1)} fusion(f32[32,1024,256]{2,1,0:T(8,128)} %convolution_bitcast_fusion, f32[1024]{0:T(1024)S(1)} %bitcast.80, f32[1024]{0:T(1024)S(1)} %bitcast.77, f32[1024]{0:T(1024)S(1)} %bitcast.78, f32[1024]{0:T(1024)S(1)} %bitcast.79, f32[1024]{0:T(1024)S(1)} %bitcast.76), kind=kLoop, calls=%fused_computation | loop fusion | flops 83886080 | bytes 50352128 | tf_op jit(solution)/shard_map/convert_element_type | solution.py:64
  421.4 15.8 copy.14
  437.2 369.5 %all_to_all.72 = bf16[32,1024,256]{2,0,1:T(8,128)(2,1)S(1)} all-to-all(bf16[32,1024,256]{2,0,1:T(8,128)(2,1)S(1)} %copy.14), channel_id=1, replica_groups=mesh['lat'=4,'ch'=8] {'ch'}, dimensions={1} | all-to-all | bytes 33554432 | tf_op jit(solution)/shard_map/all_to_all | solution.py:68
  813.4 13.9 convolution_convert_fusion.2
  827.4 17.9 %copy.16 = bf16[256,128,256]{2,1,0:T(8,128)(2,1)} copy(bf16[256,128,256]{2,0,1:T(8,128)(2,1)} %convolution_convert_fusion.2) | data formatting | bytes 33554432 | tf_op jit(solution)/shard_map/convert_element_type | solution.py:70
  851.3 17.5 %fusion.86 = bf16[1024,1024,1]{1,0,2:T(8,128)(2,1)S(1)} fusion(s32[1024]{0:T(1024)S(1)} %get-tuple-element.10, s32[1024]{0:T(1024)S(1)} %get-tuple-element.11, pred[]{:T(512)S(6)} %eq.32), kind=kLoop, calls=%fused_computation.35.clone.clone.1 | loop fusion | flops 17825792 | bytes 2105345 | tf_op jit(solution)/shard_map/fnb,wn->fbw/dot_general | solution.py:72
  868.8 344.4 %all-to-all-done.2 = bf16[256,128,256]{2,1,0:T(8,128)(2,1)} async-done(((bf16[256,128,256]{2,1,0:T(8,128)(2,1)}), bf16[256,128,256]{2,1,0:T(8,128)(2,1)}, u32[]{:S(2)}, u32[]{:S(2)}) %all-to-all-start.2) | async-done | bytes 16777248 | tf_op jit(solution)/shard_map/all_to_all | solution.py:71
  1213.2 23.4 %copy.17 = bf16[8,32,128,256]{2,0,3,1:T(8,128)(2,1)} copy(bf16[8,32,128,256]{3,2,1,0:T(8,128)(2,1)} %bitcast.16) | data formatting | bytes 33554432 | tf_op jit(solution)/shard_map/all_to_all | solution.py:71
  1236.6 25.3 %all_to_all.63 = bf16[32,1024,256]{1,2,0:T(8,128)(2,1)} reshape(bf16[32,8,128,256]{2,1,3,0:T(8,128)(2,1)} %bitcast.74) | data formatting | bytes 33554432 | tf_op jit(solution)/shard_map/all_to_all | solution.py:71
  1261.9 26.1 %convolution_convert_fusion.1 = bf16[32,256,1024]{2,1,0:T(8,128)(2,1)} fusion(bf16[32,1024,256]{1,2,0:T(8,128)(2,1)} %all_to_all.63, bf16[1024,1024,1]{1,0,2:T(8,128)(2,1)S(1)} %fusion.86), kind=kOutput, calls=%fused_computation.11 | convolution fusion | flops 17188257792 | bytes 35651584 | tf_op jit(solution)/shard_map/fnb,wn->fbw/dot_general | solution.py:72
  1288.0 23.9 %copy.18 = bf16[32,256,1024]{1,0,2:T(8,128)(2,1)} copy(bf16[32,256,1024]{2,1,0:T(8,128)(2,1)} %convolution_convert_fusion.1) | data formatting | bytes 33554432 | tf_op jit(solution)/shard_map/convert_element_type | solution.py:74
  1319.1 34.9 %fusion.80 = bf16[2048,1024,1]{1,0,2:T(8,128)(2,1)} fusion(f32[1024]{0:T(1024)S(1)} %select_multiply_fusion, s32[1024]{0:T(1024)S(1)} %copy-done.4, pred[1024]{0:T(1024)(128)(4,1)S(1)} %copy-done.6), kind=kLoop, calls=%fused_computation.31.clone.clone.1 | loop fusion | flops 35651584 | bytes 4203520 | tf_op jit(solution)/shard_map/ckr,nk->crn/dot_general | solution.py:78
  1354.0 148.1 %all-to-all-done.3 = bf16[32,256,1024]{1,0,2:T(8,128)(2,1)} async-done(((bf16[32,256,1024]{1,0,2:T(8,128)(2,1)}), bf16[32,256,1024]{1,0,2:T(8,128)(2,1)}, u32[]{:S(2)}, u32[]{:S(2)}) %all-to-all-start.3) | async-done | bytes 16777248 | tf_op jit(solution)/shard_map/all_to_all | solution.py:75
  1502.1 22.3 %copy.26 = bf16[32,256,4,256]{1,2,3,0:T(4,128)(2,1)} copy(bf16[32,256,4,256]{1,0,3,2:T(8,128)(2,1)} %bitcast.19) | data formatting | bytes 33554432 | tf_op jit(solution)/shard_map/all_to_all | solution.py:75
  1524.3 27.3 %all_to_all.67 = bf16[32,1024,256]{1,2,0:T(8,128)(2,1)} reshape(bf16[32,4,256,256]{2,1,3,0:T(4,128)(2,1)} %bitcast.75) | data formatting | bytes 33554432 | tf_op jit(solution)/shard_map/all_to_all | solution.py:75
  1551.7 45.6 %convolution_convert_fusion = bf16[32,256,2048]{2,1,0:T(8,128)(2,1)} fusion(bf16[32,1024,256]{1,2,0:T(8,128)(2,1)} %all_to_all.67, bf16[2048,1024,1]{1,0,2:T(8,128)(2,1)} %fusion.80), kind=kOutput, calls=%fused_computation.3 | convolution fusion | flops 34376515584 | bytes 54525952 | tf_op jit(solution)/shard_map/ckr,nk->crn/dot_general | solution.py:78
  (23 shorter events, 28.1 us)
Async XLA Ops:
  0.0 813.4 %copy-start = (bf16[2,256,256]{2,1,0:T(8,128)(2,1)S(1)}, bf16[2,256,256]{2,1,0:T(8,128)(2,1)}, u32[]{:S(2)}) copy-start(bf16[2,256,256]{2,1,0:T(8,128)(2,1)} %param.5) | copy-start | bytes 786436
  0.0 0.6 copy-start.3
  0.6 0.6 copy-start.5
  96.4 7.2 copy-start.2
  96.4 190.8 %all-to-all-start = ((bf16[32,1024,256]{2,0,1:T(8,128)(2,1)}), bf16[32,1024,256]{2,0,1:T(8,128)(2,1)}, u32[]{:S(2)}, u32[]{:S(2)}) async-start(bf16[32,1024,256]{2,0,1:T(8,128)(2,1)} %copy.11), calls=%async_computation | async-start | bytes 33554432 | tf_op jit(solution)/shard_map/all_to_all | solution.py:60
  845.3 367.9 %all-to-all-start.2 = ((bf16[256,128,256]{2,1,0:T(8,128)(2,1)}), bf16[256,128,256]{2,1,0:T(8,128)(2,1)}, u32[]{:S(2)}, u32[]{:S(2)}) async-start(bf16[256,128,256]{2,1,0:T(8,128)(2,1)} %copy.16), calls=%async_computation.2 | async-start | bytes 33554432 | tf_op jit(solution)/shard_map/all_to_all | solution.py:71
  1311.9 7.1 copy-start.4
  1312.0 7.1 copy-start.6
  1312.0 190.1 %all-to-all-start.3 = ((bf16[32,256,1024]{1,0,2:T(8,128)(2,1)}), bf16[32,256,1024]{1,0,2:T(8,128)(2,1)}, u32[]{:S(2)}, u32[]{:S(2)}) async-start(bf16[32,256,1024]{1,0,2:T(8,128)(2,1)} %copy.18), calls=%async_computation.3 | async-start | bytes 33554432 | tf_op jit(solution)/shard_map/all_to_all | solution.py:75
  1551.7 45.6 %copy-start.1 = (bf16[2,256,256]{2,1,0:T(8,128)(2,1)S(1)}, bf16[2,256,256]{2,1,0:T(8,128)(2,1)}, u32[]{:S(2)}) copy-start(bf16[2,256,256]{2,1,0:T(8,128)(2,1)} %param.5) | copy-start | bytes 786436
where the time goes:
time: 1610 us; the launch traced here: 1600 us
  waiting for transfers between devices  659 us (41%)
  blocking collectives  370 us (23%)
  local copies, waits for them, and re-layouts  232 us (14%)
  other arithmetic  164 us (10%)
  matrix products  153 us (10%)
  starting transfers between devices  20.2 us (1%)
    all_to_all x1, blocking collectives, per_device(): lax.all_to_all(converted, 'ch', split_axis=1, concat_axis=0, tiled=True)  370 us
    all_to_all x1, waiting for transfers between devices, per_device(): lax.all_to_all(mixed, 'ch', split_axis=0, concat_axis=1, tiled=True)  344 us
    all_to_all x1, waiting for transfers between devices, per_device(): lax.all_to_all(spectra, 'lat', split_axis=1, concat_axis=2, tiled=True)  166 us
    all_to_all x1, waiting for transfers between devices, per_device(): lax.all_to_all(lat_rows, 'lat', split_axis=2, concat_axis=1, tiled=True)  148 us
    convert_element_type x1, other arithmetic, per_device(): converted = convert(amplitudes, coeffs).astype(jnp.bfloat16)  59.1 us
    all_to_all x2, local copies, waits for them, and re-layouts, per_device(): lax.all_to_all(lat_rows, 'lat', split_axis=2, concat_axis=1, tiled=True)  49.6 us
    all_to_all x2, local copies, waits for them, and re-layouts, per_device(): lax.all_to_all(spectra, 'lat', split_axis=1, concat_axis=2, tiled=True)  49.6 us
    all_to_all x2, local copies, waits for them, and re-layouts, per_device(): lax.all_to_all(mixed, 'ch', split_axis=0, concat_axis=1, tiled=True)  48.7 us
  transfers between devices with their start and end apart: 3, of which 3 were waited for; matrix products, arithmetic and copies ran while one was open for 4% of the time, Pallas kernels for 0%

commit v1 on v0

v1 whole, which is shorter than its diff:
```python
import functools
import math

import jax
import jax.numpy as jnp
import numpy as np
from jax import lax
from jax.experimental import pallas as pl
from jax.experimental.pallas import tpu as pltpu
from jax.sharding import PartitionSpec as P

AXES = ("lat", "ch")
CHUNKS = 2


def lon_half(cols, nlon):
    km = cols // 2
    column = np.arange(cols)
    mode = 2 * (column % (km // 2)) + column // km
    phase = (np.arange(nlon // 2)[:, None] * mode[None, :] % nlon) * (2.0 * math.pi / nlon)
    cosine = (column % km // (km // 2) == 0)[None, :]
    table = np.where(cosine, np.cos(phase), np.sin(phase)) / math.sqrt(nlon)
    return table.astype(jnp.bfloat16), np.where(mode == 0, 1.0, 2.0).astype(jnp.bfloat16)


def lat_table(parity, nlat, kl):
    rows = jnp.arange(nlat, dtype=jnp.int32)
    waves = jnp.arange(kl, dtype=jnp.int32) + parity
    angles = ((2 * rows[:, None] + 1) * waves[None, :] % (4 * nlat)).astype(jnp.float32)
    angles = angles * (math.pi / (2 * nlat))
    table = jnp.where(parity == 0, jnp.cos(angles), jnp.sin(angles))
    return (table * math.sqrt(2.0 / nlat)).astype(jnp.bfloat16)


def lon_inverse_kernel(chunks, *refs):
    blocks, table, out = refs[:chunks], refs[chunks], refs[chunks + 1]
    nd, _, kc, rows = blocks[0].shape
    half = out.shape[2] // 2
    sums = []
    for p in range(2):
        total = None
        for j in range(chunks):
            x = blocks[j][p * (nd // 2) : (p + 1) * (nd // 2), 0].reshape(nd // 2 * kc, rows)
            part = lax.dot_general(
                x, table[j, p], (((0,), (0,)), ((), ())), preferred_element_type=jnp.float32
            )
            total = part if total is None else total + part
        sums.append(total)
    out[0, :, :half] = (sums[0] + sums[1]).astype(out.dtype)
    out[0, :, half:] = (sums[0] - sums[1]).astype(out.dtype)


def lon_inverse(back, inverse, nlon):
    chunks = len(back)
    nd, c, kc, rows = back[0].shape
    table = inverse.reshape(nlon // 2, 2, nd // 2, chunks, kc).transpose(3, 1, 2, 4, 0)
    table = table.reshape(chunks, 2, nd // 2 * kc, nlon // 2)
    if kc % 16 == 0:
        return pl.pallas_call(
            functools.partial(lon_inverse_kernel, chunks),
            grid=(c,),
            in_specs=[pl.BlockSpec((nd, 1, kc, rows), lambda i: (0, i, 0, 0))] * chunks
            + [pl.BlockSpec(table.shape, lambda i: (0, 0, 0, 0))],
            out_specs=pl.BlockSpec((1, rows, nlon), lambda i: (i, 0, 0)),
            out_shape=jax.ShapeDtypeStruct((c, rows, nlon), jnp.bfloat16),
            compiler_params=pltpu.CompilerParams(vmem_limit_bytes=48 << 20),
            cost_estimate=pl.CostEstimate(
                flops=2 * c * rows * nlon * nd * kc * chunks // 2,
                bytes_accessed=2 * c * rows * (nlon + nd * kc * chunks),
                transcendentals=0,
            ),
        )(*back, table)
    x = jnp.stack(back).reshape(chunks, 2, nd // 2, c, kc, rows)
    t = table.reshape(chunks, 2, nd // 2, kc, nlon // 2)
    even, odd = (
        jnp.einsum("jdckr,jdkn->crn", x[:, p], t[:, p], preferred_element_type=jnp.float32) for p in range(2)
    )
    return jnp.concatenate([even + odd, even - odd], 2).astype(jnp.bfloat16)


def per_device(field, band, mixing):
    nl, nc = lax.axis_size("lat"), lax.axis_size("ch")
    nd = nl * nc
    c, rows, nlon = field.shape
    nlat, kl = rows * nl, band.shape[2]
    cols = nlon // 2
    km = cols // 2
    share = cols // nd
    chunks = CHUNKS if share % CHUNKS == 0 else 1
    kc = share // chunks
    me = lax.axis_index("lat") * nc + lax.axis_index("ch")
    parity = me * share // km

    half, weight = lon_half(cols, nlon)
    half = jnp.asarray(half)
    sign = jnp.where(jnp.arange(cols) < km, 1.0, -1.0).astype(jnp.bfloat16)
    forward = jnp.concatenate([half, half * sign], 0).reshape(nlon, nd, chunks, kc)

    sent = []
    for j in range(chunks):
        spectra = jnp.einsum("crn,ndk->dkcr", field, forward[:, :, j], preferred_element_type=jnp.float32)
        sent.append(lax.all_to_all(spectra.astype(jnp.bfloat16), AXES, 0, 0, tiled=True))

    table = lat_table(parity, nlat, kl)
    coeffs = lax.dynamic_index_in_dim(band, parity, 0, keepdims=False)
    weights = lax.dynamic_index_in_dim(mixing, parity, 0, keepdims=False)
    padded = jnp.pad(table.astype(jnp.float32), ((0, 0), (2, 2)))
    conv = sum(coeffs[s][None, :] * padded[:, s : s + kl] for s in range(5))
    kernel = jnp.einsum("rl,ql->rq", conv.astype(jnp.bfloat16), table, preferred_element_type=jnp.float32)
    kernel = kernel.astype(jnp.bfloat16).reshape(nl, rows, nl, rows)

    back = []
    for j in range(chunks):
        got = sent[j].reshape(nl, nc, kc, c, rows)
        w = weights.reshape(nc * c, nc, c)
        mixed = jnp.einsum("ojc,ijkcr->kior", w, got, preferred_element_type=jnp.float32).astype(jnp.bfloat16)
        z = jnp.einsum("kior,irsq->skoq", mixed, kernel, preferred_element_type=jnp.float32).astype(jnp.bfloat16)
        z = z.reshape(nl, kc, nc, c, rows).transpose(0, 2, 3, 1, 4).reshape(nd, c, kc, rows)
        back.append(lax.all_to_all(z, AXES, 0, 0, tiled=True))
    return lon_inverse(back, half * jnp.asarray(weight), nlon)


def solution(mesh):
    return jax.shard_map(
        per_device,
        mesh=mesh,
        in_specs=(P("ch", "lat", None), P(), P()),
        out_specs=P("ch", "lat", None),
        check_vma=False,
    )
```

time: 1610 us -> 848 us (0.53)
  waiting for transfers between devices: 659 us -> 425 us
  local copies, waits for them, and re-layouts: 232 us -> 34.1 us
  blocking collectives: 370 us -> 189 us
  other arithmetic: 164 us -> 26 us
  matrix products: 153 us -> 112 us
  Pallas kernels: 0 us -> 36.5 us
    all_to_all x3, waiting for transfers between devices: 659 us -> 425 us  [the longest x2 271 us: per_device(): lax.all_to_all(spectra.astype(jnp.bfloat16), AXES, 0, 0, tiled=True)]
    all_to_all x1, blocking collectives: 370 us -> 189 us  [per_device(): back.append(lax.all_to_all(z, AXES, 0, 0, tiled=True))]
    all_to_all x7 -> x0, local copies, waits for them, and re-layouts: 155 us -> none  [the longest x2 49.6 us: per_device(): lax.all_to_all(lat_rows, 'lat', split_axis=2, concat_axis=1, tiled=True)]
    dot_general x4 -> x1, other arithmetic: 105 us -> 4.63 us  [per_device(): jnp.einsum('rl,ql->rq', conv.astype(jnp.bfloat16), table, preferred_eleme...]
    convert_element_type x4 -> x0, local copies, waits for them, and re-layouts: 76 us -> none  [the longest x1 23.9 us: per_device(): lat_rows = jnp.einsum('fnb,wn->fbw', channel_mixed_spectra, legendre_tabl...]
    convert_element_type x1 -> x2, other arithmetic: 59.1 us -> 17.1 us  [the longest x1 17.1 us: per_device(): padded = jnp.pad(table.astype(jnp.float32), ((0, 0), (2, 2)))]
    dot_general x5, matrix products: 153 us -> 112 us  [the longest x2 49.9 us: per_device(): jnp.einsum('crn,ndk->dkcr', field, forward[:, :, j], preferred_element_ty...]
    pallas_call x0 -> x1, Pallas kernels: none -> 36.5 us  [lon_inverse(): pl.pallas_call(functools.partial(lon_inverse_kernel, chunks), grid=(c,),...]
  transfers between devices with their start and end apart: 3 -> 3, of which waited for: 3 -> 3; matrix products, arithmetic and copies ran while one was open for 4% -> 17% of each run, Pallas kernels for 0% -> 0%
where the time goes in v1:
time: 848 us; the launch traced here: 839 us
  waiting for transfers between devices  425 us (50%)
  blocking collectives  189 us (22%)
  matrix products  112 us (13%)
  Pallas kernels  36.5 us (4%)
  local copies, waits for them, and re-layouts  34.1 us (4%)
  other arithmetic  26 us (3%)
  starting transfers between devices  15.3 us (2%)
    all_to_all x2, waiting for transfers between devices, per_device(): lax.all_to_all(spectra.astype(jnp.bfloat16), AXES, 0, 0, tiled=True)  271 us
    all_to_all x1, blocking collectives, per_device(): back.append(lax.all_to_all(z, AXES, 0, 0, tiled=True))  189 us
    all_to_all x1, waiting for transfers between devices, per_device(): back.append(lax.all_to_all(z, AXES, 0, 0, tiled=True))  154 us
    dot_general x2, matrix products, per_device(): jnp.einsum('crn,ndk->dkcr', field, forward[:, :, j], preferred_element_ty...  49.9 us
    dot_general x2, matrix products, per_device(): jnp.einsum('kior,irsq->skoq', mixed, kernel, preferred_element_type=jnp.f...  39.6 us
    pallas_call x1, Pallas kernels, lon_inverse(): pl.pallas_call(functools.partial(lon_inverse_kernel, chunks), grid=(c,),...  36.5 us
    reshape x2, local copies, waits for them, and re-layouts, per_device(): z.reshape(nl, kc, nc, c, rows).transpose(0, 2, 3, 1, 4)  30.3 us
    dot_general x1, matrix products, per_device(): jnp.einsum('rl,ql->rq', conv.astype(jnp.bfloat16), table, preferred_eleme...  23 us
  transfers between devices with their start and end apart: 3, of which 3 were waited for; matrix products, arithmetic and copies ran while one was open for 17% of the time, Pallas kernels for 0%

profile of v1, /device:TPU:0, one launch (start us, length us, event | category | flops | bytes accessed | tf_op | source)
XLA Modules:
  0.0 838.8 jit_solution(1671698451743740611)
XLA Ops:
  0.0 0.0 copy-start
  0.0 1.9 broadcast_multiply_fusion
  2.0 0.3 copy-done.2
  2.3 2.4 pad_maximum_fusion
  4.7 24.9 %fusion.16 = bf16[32,16,32,256]{3,1,2,0:T(8,128)(2,1)} fusion(bf16[32,256,2048]{2,1,0:T(8,128)(2,1)} %param.5, bf16[2048,32,2,16]{0,3,2,1:T(8,128)(2,1)} %bitcast.87), kind=kOutput, calls=%fused_computation.15 | convolution fusion | flops 17184063488 | bytes 44040192 | tf_op jit(solution)/shard_map/crn,ndk->dkcr/dot_general | solution.py:101
  29.6 7.5 all-to-all-start
  37.0 25.0 %fusion.19 = bf16[32,16,32,256]{3,1,2,0:T(8,128)(2,1)} fusion(bf16[32,256,2048]{2,1,0:T(8,128)(2,1)} %param.5, bf16[2048,32,2,16]{0,3,2,1:T(8,128)(2,1)} %bitcast.88), kind=kOutput, calls=%fused_computation.16 | convolution fusion | flops 17184063488 | bytes 44040192 | tf_op jit(solution)/shard_map/crn,ndk->dkcr/dot_general | solution.py:101
  62.0 164.8 %all-to-all-done = bf16[32,16,32,256]{3,1,2,0:T(8,128)(2,1)} async-done(((bf16[32,16,32,256]{3,1,2,0:T(8,128)(2,1)}), bf16[32,16,32,256]{3,1,2,0:T(8,128)(2,1)}, u32[]{:S(2)}, u32[]{:S(2)}) %all-to-all-start) | async-done | bytes 8388640 | tf_op jit(solution)/shard_map/all_to_all | solution.py:102
  226.8 3.9 all-to-all-start.2
  230.8 0.0 copy-done
  230.8 0.1 copy.32
  231.0 17.1 %fusion.35 = f32[1024,1024]{1,0:T(8,128)S(1)} fusion(s32[1024]{0:T(1024)S(1)} %get-tuple-element.10, s32[1024]{0:T(1024)S(1)} %get-tuple-element.11, pred[]{:T(512)S(6)} %eq.5), kind=kLoop, calls=%fused_computation.40 | loop fusion | flops 18874368 | bytes 4202497 | tf_op jit(solution)/shard_map/convert_element_type | solution.py:107
  248.1 4.6 fusion.53
  252.7 23.0 %fusion.37 = bf16[1024,1024]{1,0:T(8,128)(2,1)} fusion(s32[1024]{0:T(1024)S(1)} %get-tuple-element.10, s32[1024]{0:T(1024)S(1)} %get-tuple-element.11, pred[]{:T(512)S(6)} %eq.5, bf16[1024,1024]{1,0:T(8,128)(2,1)S(1)} %fusion.53), kind=kOutput, calls=%fused_computation.41 | convolution fusion | flops 2166358016 | bytes 4202497 | tf_op jit(solution)/shard_map/rl,ql->rq/dot_general | solution.py:109
  275.7 3.3 reshape.63
  279.0 19.9 %bitcast_convert_fusion.2 = bf16[4,256,16,256]{1,3,2,0:T(8,128)(2,1)} fusion(bf16[256,8,32,1,1]{0,2,1,3,4:T(8,128)(2,1)S(1)} %bitcast.91, bf16[4,8,16,32,256]{4,2,3,1,0:T(8,128)(2,1)} %bitcast.11, bf16[4,256,4,256,1]{3,2,1,0,4:T(4,128)(2,1)S(1)} %bitcast.89), kind=kOutput, calls=%fused_computation.6 | convolution fusion | flops 10745806848 | bytes 19005440 | tf_op jit(solution)/shard_map/kior,irsq->skoq/dot_general | solution.py:117
  298.9 15.1 %copy.13 = bf16[4,16,8,32,256]{4,1,3,2,0:T(8,128)(2,1)} copy(bf16[4,16,8,32,256]{4,3,2,1,0:T(8,128)(2,1)} %bitcast.86) | data formatting | bytes 16777216 | tf_op jit(solution)/shard_map/reshape | solution.py:118
  314.0 106.2 %all-to-all-done.2 = bf16[32,16,32,256]{3,1,2,0:T(8,128)(2,1)} async-done(((bf16[32,16,32,256]{3,1,2,0:T(8,128)(2,1)}), bf16[32,16,32,256]{3,1,2,0:T(8,128)(2,1)}, u32[]{:S(2)}, u32[]{:S(2)}) %all-to-all-start.2) | async-done | bytes 8388640 | tf_op jit(solution)/shard_map/all_to_all | solution.py:102
  420.2 3.9 all-to-all-start.1
  424.1 19.8 %bitcast_convert_fusion = bf16[4,256,16,256]{1,3,2,0:T(8,128)(2,1)} fusion(bf16[256,8,32,1,1]{0,2,1,3,4:T(8,128)(2,1)S(1)} %bitcast.92, bf16[4,8,16,32,256]{4,2,3,1,0:T(8,128)(2,1)} %bitcast.28, bf16[4,256,4,256,1]{3,2,1,0,4:T(4,128)(2,1)S(1)} %bitcast.90), kind=kOutput, calls=%fused_computation.4 | convolution fusion | flops 10745806848 | bytes 19005440 | tf_op jit(solution)/shard_map/kior,irsq->skoq/dot_general | solution.py:117
  443.9 15.2 %copy.16 = bf16[4,16,8,32,256]{4,1,3,2,0:T(8,128)(2,1)} copy(bf16[4,16,8,32,256]{4,3,2,1,0:T(8,128)(2,1)} %bitcast.85) | data formatting | bytes 16777216 | tf_op jit(solution)/shard_map/reshape | solution.py:118
  459.1 154.2 %all-to-all-done.1.refs_0_ = bf16[32,32,16,256]{3,2,1,0:T(8,128)(2,1)} async-done(((bf16[32,32,16,256]{3,2,1,0:T(8,128)(2,1)}), bf16[32,32,16,256]{3,2,1,0:T(8,128)(2,1)}, u32[]{:S(2)}, u32[]{:S(2)}) %all-to-all-start.1) | async-done | bytes 8388640 | tf_op jit(solution)/shard_map/all_to_all | solution.py:119
  613.3 188.6 %all_to_all.20.refs_1_ = bf16[32,32,16,256]{3,2,1,0:T(8,128)(2,1)} all-to-all(bf16[32,32,16,256]{3,2,1,0:T(8,128)(2,1)} %bitcast.84), channel_id=1, replica_groups=mesh['lat'=4,'ch'=8] {'lat','ch'}, dimensions={0} | all-to-all | bytes 16777216 | tf_op jit(solution)/shard_map/all_to_all | solution.py:119
  801.9 36.5 %shard_map.55 = bf16[32,256,2048]{2,1,0:T(8,128)(2,1)} custom-call(bf16[32,32,16,256]{3,2,1,0:T(8,128)(2,1)} %all-to-all-done.1.refs_0_, bf16[32,32,16,256]{3,2,1,0:T(8,128)(2,1)} %all_to_all.20.refs_1_, bf16[2,2,256,1024]{3,2,1,0:T(8,128)(2,1)S(1)} %copy-done.1), custom_call_target="tpu_custom_call" | custom-call | flops 17179869184 | bytes 50331648 | tf_op jit(solution)/shard_map/pallas_call | solution.py:59
  (9 shorter events, 0.1 us)
Async XLA Ops:
  0.0 230.8 %copy-start = (bf16[2,256,256]{2,1,0:T(8,128)(2,1)S(1)}, bf16[2,256,256]{2,1,0:T(8,128)(2,1)}, u32[]{:S(2)}) copy-start(bf16[2,256,256]{2,1,0:T(8,128)(2,1)} %param.7) | copy-start | bytes 786436
  0.0 2.3 copy-start.2
  29.6 197.3 %all-to-all-start = ((bf16[32,16,32,256]{3,1,2,0:T(8,128)(2,1)}), bf16[32,16,32,256]{3,1,2,0:T(8,128)(2,1)}, u32[]{:S(2)}, u32[]{:S(2)}) async-start(bf16[32,16,32,256]{3,1,2,0:T(8,128)(2,1)} %fusion.16), calls=%async_computation | async-start | bytes 16777216 | tf_op jit(solution)/shard_map/all_to_all | solution.py:102
  62.0 169.0 %copy-start.3 = (f32[2,5,1024]{2,0,1:T(2,128)S(1)}, f32[2,5,1024]{2,0,1:T(2,128)}, u32[]{:S(2)}) copy-start(f32[2,5,1024]{2,0,1:T(2,128)} %param.6) | copy-start | bytes 122884
  226.8 193.3 %all-to-all-start.2 = ((bf16[32,16,32,256]{3,1,2,0:T(8,128)(2,1)}), bf16[32,16,32,256]{3,1,2,0:T(8,128)(2,1)}, u32[]{:S(2)}, u32[]{:S(2)}) async-start(bf16[32,16,32,256]{3,1,2,0:T(8,128)(2,1)} %fusion.19), calls=%async_computation.2 | async-start | bytes 16777216 | tf_op jit(solution)/shard_map/all_to_all | solution.py:102
  420.2 193.1 %all-to-all-start.1 = ((bf16[32,32,16,256]{3,2,1,0:T(8,128)(2,1)}), bf16[32,32,16,256]{3,2,1,0:T(8,128)(2,1)}, u32[]{:S(2)}, u32[]{:S(2)}) async-start(bf16[32,32,16,256]{3,2,1,0:T(8,128)(2,1)} %bitcast.83), calls=%async_computation.1 | async-start | bytes 16777216 | tf_op jit(solution)/shard_map/all_to_all | solution.py:119
  613.3 188.6 %copy-start.1 = (bf16[2,2,256,1024]{3,2,1,0:T(8,128)(2,1)S(1)}, bf16[2,2,256,1024]{3,2,1,0:T(8,128)(2,1)}, u32[]{:S(2)}) copy-start(bf16[2,2,256,1024]{3,2,1,0:T(8,128)(2,1)} %constant.77.refs_2_) | copy-start | bytes 6291460
